TPU v7x, 128 devices: a whole 4x4x4 slice. The times are simulated.
128 devices in a mesh: row: 8 (over z, core), col: 16 (over y, x).
Axes of the slice: x: 4, y: 4, z: 4, core: 2. Of those that a mesh axis runs over, the one named last changes fastest.
Arguments:
- hidden: bfloat16 [1408, 16384], P('col', 'row'), may hold values from -18 to 18
- gain_in: bfloat16 [1408], replicated, may hold values from 0.5 to 1.5
- w_query: bfloat16 [1408, 1408], P('col'), may hold values from -0.3125 to 0.3125
- w_pair: bfloat16 [2, 1408, 1408], P(None, 'col'), may hold values from -0.15625 to 0.15625
- kv_cache: bfloat16 [2, 1408, 16384], P(None, 'col', 'row'), may hold values from -103 to 103
- recompute_rows: int32 [8, 200], P('row'), may hold values from 0 to 2047, as said below
- segment_ids: int32 [16384], P('row'), may hold values from -1 to 1, as said below
- w_out: bfloat16 [1408, 1408], P('col'), may hold values from -0.3125 to 0.3125
- gain_merge: bfloat16 [1408], replicated, may hold values from 0.5 to 1.5
- w_merge: bfloat16 [4, 1408, 1408], P(None, 'col'), may hold values from -0.078125 to 0.078125
- requests: int32 [8, 16, 85], P('row'), may hold values from -1 to 511, as said below
Outputs:
- delivered: bfloat16 [8, 16, 85, 1408], P('row', 'col')
Inputs may be any that keep to these rules, and one draw needn't show every extreme that they name: `segment_ids`: ids do not fall along the tokens except to -1 for the padding at the end; every image covers a multiple of 4 tokens and starts at a multiple of 4. `recompute_rows`: the 200 offsets of one index of row are distinct. `requests`: for each index of row, the lists of all owners together name each of its 512 merged tokens exactly once; unused slots hold -1 and follow the used ones.
All inputs are finite; a program needn't handle non-finite values.
Results may differ from a plain program's by a relative error of at most 0.025.
The roundings to bfloat16 on the way count: a program that leaves them out, or rounds other values in their place, can miss the bound.
Values may be sent and summed in bfloat16 or wider, within the bound.
A program may use at most 128 MiB of HBM per device.

v0:
```python
import jax
import jax.numpy as jnp
from jax import lax
from jax.sharding import PartitionSpec as P

HD = 88
EPSILON = 1e-06
MASKED = -1e30
KEY_BLOCK = 1024


def on_device(
    hidden,
    gain_in,
    w_query,
    w_pair,
    kv_cache,
    recompute_rows,
    segment_ids,
    w_out,
    gain_merge,
    w_merge,
    requests,
):
    local_width, tok_rows = hidden.shape
    model_width = w_query.shape[1]
    n_col = model_width // local_width
    heads_here = local_width // HD
    score_scale = HD ** (-0.5)
    col_index = lax.axis_index("col")
    full_rows = lax.all_gather(hidden, "col", axis=0, tiled=True)
    out_weight = lax.all_gather(w_out, "col", axis=0, tiled=True)
    full_float = full_rows.astype(jnp.float32)
    in_mean = jnp.sum(full_float, axis=0, keepdims=True) / model_width
    in_square = jnp.sum(full_float * full_float, axis=0, keepdims=True) / model_width
    normed = (
        (full_float - in_mean)
        * lax.rsqrt(in_square - in_mean * in_mean + EPSILON)
        * gain_in.astype(jnp.float32)[:, None]
    ).astype(jnp.bfloat16)
    queries = jnp.dot(w_query, normed, preferred_element_type=jnp.float32).astype(jnp.bfloat16)
    picked_rows = recompute_rows[0]
    normed_picked = jnp.take(normed, picked_rows, axis=1)
    fresh_pairs = jnp.dot(
        w_pair.reshape(2 * local_width, model_width),
        normed_picked,
        preferred_element_type=jnp.float32,
    )
    fresh_pairs = fresh_pairs.astype(jnp.bfloat16).reshape(2, local_width, -1)
    keys_values = kv_cache.at[:, :, picked_rows].set(fresh_pairs)
    query_heads = queries.reshape(heads_here, HD, tok_rows)
    pair_local = jnp.concatenate(
        [keys_values.reshape(2 * local_width, tok_rows), segment_ids.astype(jnp.bfloat16)[None, :]],
        axis=0,
    )
    pair_all = lax.all_gather(pair_local, "row", axis=1, tiled=True)
    pair_rows = pair_all[: 2 * local_width].reshape(2, local_width, -1)
    segment_line = pair_all[2 * local_width].astype(jnp.int32)

    def take_block(carried, pair_block, segment_block):
        running_max, running_sum, weighted = carried
        key_block = pair_block[0].reshape(heads_here, HD, -1)
        value_block = pair_block[1].reshape(heads_here, HD, -1)
        scores = (
            jnp.einsum("hdq,hdk->hqk", query_heads, key_block, preferred_element_type=jnp.float32)
            * score_scale
        )
        allowed = (segment_ids[:, None] == segment_block[None, :])[None, :, :]
        new_max = jnp.maximum(running_max, jnp.max(jnp.where(allowed, scores, MASKED), axis=2))
        weights_exp = jnp.where(allowed, jnp.exp(scores - new_max[:, :, None]), 0.0)
        factor = jnp.exp(running_max - new_max)
        running_sum = running_sum * factor + jnp.sum(weights_exp, axis=2)
        product = jnp.einsum(
            "hqk,hdk->hdq",
            weights_exp.astype(jnp.bfloat16),
            value_block,
            preferred_element_type=jnp.float32,
        )
        weighted = weighted * factor[:, None, :] + product
        return (new_max, running_sum, weighted)

    starting = (
        jnp.full((heads_here, tok_rows), MASKED, jnp.float32),
        jnp.zeros((heads_here, tok_rows), jnp.float32),
        jnp.zeros((heads_here, HD, tok_rows), jnp.float32),
    )
    piece_rows = pair_rows.shape[2]
    whole_blocks = piece_rows // KEY_BLOCK

    def loop_body(block_index, loop_state):
        pair_block = lax.dynamic_slice_in_dim(pair_rows, block_index * KEY_BLOCK, KEY_BLOCK, 2)
        segment_block = lax.dynamic_slice_in_dim(
            segment_line, block_index * KEY_BLOCK, KEY_BLOCK, 0
        )
        return take_block(loop_state, pair_block, segment_block)

    running_max, running_sum, weighted = lax.fori_loop(0, whole_blocks, loop_body, starting)
    attended = (
        (weighted / running_sum[:, None, :]).astype(jnp.bfloat16).reshape(local_width, tok_rows)
    )
    chunk = tok_rows // n_col
    attended_chunk = lax.all_to_all(attended, "col", 1, 0, tiled=True)
    x_chunk = lax.dynamic_slice_in_dim(full_float, col_index * chunk, chunk, 1)
    projected = lax.dot_general(
        out_weight, attended_chunk, (((0,), (0,)), ((), ())), preferred_element_type=jnp.float32
    )
    updated = x_chunk + projected
    row_mean = jnp.sum(updated, axis=0, keepdims=True) / model_width
    row_square = jnp.sum(updated * updated, axis=0, keepdims=True) / model_width
    merger_chunk = (
        (updated - row_mean)
        * lax.rsqrt(row_square - row_mean * row_mean + EPSILON)
        * gain_merge.astype(jnp.float32)[:, None]
    ).astype(jnp.bfloat16)
    merge_weight, _ = lax.optimization_barrier((w_merge, pair_all))
    merge_full = lax.all_gather(merge_weight, "col", axis=1, tiled=True)
    grouped = merger_chunk.reshape(model_width, chunk // 4, 4)
    merged_here = jnp.einsum("fgi,ifd->gd", grouped, merge_full, preferred_element_type=jnp.float32)
    merged_all = lax.all_gather(merged_here.astype(jnp.bfloat16), "col", axis=0, tiled=True)
    wanted_rows = lax.dynamic_index_in_dim(requests[0], col_index, 0, keepdims=False)
    is_valid = wanted_rows >= 0
    safe_index = jnp.where(is_valid, wanted_rows, 0)
    picked = jnp.where(is_valid[:, None], merged_all[safe_index], jnp.zeros((), jnp.bfloat16))
    return picked.reshape(1, 1, picked.shape[0], model_width)


def solution(mesh):
    placed = (
        P("col", "row"),
        P(),
        P("col", None),
        P(None, "col", None),
        P(None, "col", "row"),
        P("row", None),
        P("row"),
        P("col", None),
        P(),
        P(None, "col", None),
        P("row", None, None),
    )
    return jax.shard_map(
        on_device,
        mesh=mesh,
        in_specs=placed,
        out_specs=P("row", "col", None, None),
        check_vma=False,
    )
```

profile of v0, /device:TPU:0, one launch (start us, length us, event | category | flops | bytes accessed | tf_op | source)
XLA Modules:
  0.0 484.3 jit_solution(13265763063287293929)
XLA Ops:
  12.5 58.2 %all-gather.6.cloned.1.call-done = bf16[1408,2048]{1,0:T(8,128)(2,1)} async-done(((bf16[88,2048]{1,0:T(8,128)(2,1)}), bf16[1408,2048]{1,0:T(8,128)(2,1)}) %all-gather.6.cloned.1.call-update) | async-done | bytes 5767184 | tf_op jit(solution)/shard_map/all_gather | solution.py:31
  70.7 8.3 %copy.28 = bf16[1408,2048]{0,1:T(8,128)(2,1)} copy(bf16[1408,2048]{1,0:T(8,128)(2,1)} %all-gather.6.cloned.1.call-done) | data formatting | bytes 11534336 | tf_op jit(solution)/shard_map/all_gather | solution.py:31
  87.6 5.0 %gather_fusion = bf16[200,1408]{1,0:T(8,128)(2,1)S(1)} fusion(bf16[1408,2048]{0,1:T(8,128)(2,1)} %multiply_convert_fusion, s32[1024]{0:T(1024)S(1)} %pad_clamp_fusion.1), kind=kCustom, calls=%fused_computation | custom fusion | bytes 1127200 | tf_op jit(solution)/shard_map/jit(_take)/gather | solution.py:43
  93.2 6.9 %scatter_fusion = bf16[2,88,2048]{1,0,2:T(2,128)(2,1)S(1)} fusion(bf16[2,88,2048]{1,0,2:T(2,128)(2,1)S(1)} %copy.30, s32[200]{0:T(256)S(1)} %bitcast.122, bf16[200,2,88]{2,1,0:T(2,128)(2,1)S(1)} %bitcast.115), kind=kCustom, calls=%fused_computation.2 | custom fusion | bytes 212000 | tf_op jit(solution)/shard_map/scatter | solution.py:50
  107.5 34.2 %all-gather.8.cloned.1.call-done = bf16[177,16384]{1,0:T(8,128)(2,1)} async-done(((bf16[177,2048]{1,0:T(8,128)(2,1)}), bf16[177,16384]{1,0:T(8,128)(2,1)}) %all-gather.8.cloned.1.call-update) | async-done | bytes 5799952 | tf_op jit(solution)/shard_map/all_gather | solution.py:56
  141.7 5.8 %slice.29 = bf16[176,16384]{1,0:T(8,128)(2,1)} slice(bf16[177,16384]{1,0:T(8,128)(2,1)} %all-gather.8.cloned.1.call-done), slice={[0:176], [0:16384]} | slice | bytes 11534336 | tf_op jit(solution)/shard_map/slice | solution.py:57
  148.5 254.0 %while.18 = (s32[]{:T(128)}, f32[1,2048]{1,0:T(1,128)S(1)}, f32[1,2048]{1,0:T(1,128)S(1)}, f32[1,88,2048]{2,1,0:T(8,128)S(1)}, s32[2048]{0:T(1024)S(1)}, /*index...) while((s32[]{:T(128)}, f32[1,2048]{1,0:T(1,128)S(1)}, ...), condition=%wide.region_6.7_spmd.clone, body=%wide.region_3.0_spmd.clone.sunk | while | flops 768108544 | bytes 27504848 | solution.py:97
  148.5 5.6 %fusion.45 = (f32[2048]{0:T(1024)S(1)}, f32[1024,2048]{1,0:T(8,128)}) fusion(s32[2048]{0:T(1024)S(1)} %get-tuple-element.292, s32[1024]{0:T(1024)S(1)} %dynamic_slice.32, bf16[1,88,2048]{2,1,0:T(8,128)(2,1)S(1)} %get-tuple-element.295, bf16[2,88,16384]{2,1,0:T(8,128)(2,1)} %get-tuple-element.294, s32[]{:T(128)S(6)} %select_n.132), kind=kOutput, calls=%fused_computation.5.clone.1 | convolution fusion | flops 377485312 | bytes 8949764 | tf_op jit(solution)/shard_map/while/body/eval_jaxpr/hdq,hdk->hqk/dot_general | solution.py:65
  158.8 5.5 %fusion.49 = f32[1,88,2048]{2,1,0:T(8,128)S(1)} fusion(f32[1024,2048]{1,0:T(8,128)} %get-tuple-element.259, f32[2048]{0:T(1024)S(1)} %bitcast.110, s32[2048]{0:T(1024)S(1)} %get-tuple-element.292, s32[1024]{0:T(1024)S(1)} %dynamic_slice.32, f32[1,88,2048]{2,1,0:T(8,128)S(1)} %get-tuple-element.278, f32[2048]{0:T(1024)S(1)} %bitcast.117, ...), kind=kOutput, calls=%fused_computation.12.clone.1 | convolution fusion | flops 380125184 | bytes 10039305 | tf_op jit(solution)/shard_map/while/body/eval_jaxpr/hqk,hdk->hdq/dot_general | solution.py:73
  164.3 5.6 %fusion.45 = (f32[2048]{0:T(1024)S(1)}, f32[1024,2048]{1,0:T(8,128)}) fusion(s32[2048]{0:T(1024)S(1)} %get-tuple-element.292, s32[1024]{0:T(1024)S(1)} %dynamic_slice.32, bf16[1,88,2048]{2,1,0:T(8,128)(2,1)S(1)} %get-tuple-element.295, bf16[2,88,16384]{2,1,0:T(8,128)(2,1)} %get-tuple-element.294, s32[]{:T(128)S(6)} %select_n.132), kind=kOutput, calls=%fused_computation.5.clone.1 | convolution fusion | flops 377485312 | bytes 8949764 | tf_op jit(solution)/shard_map/while/body/eval_jaxpr/hdq,hdk->hqk/dot_general | solution.py:65
  174.5 5.4 %fusion.49 = f32[1,88,2048]{2,1,0:T(8,128)S(1)} fusion(f32[1024,2048]{1,0:T(8,128)} %get-tuple-element.259, f32[2048]{0:T(1024)S(1)} %bitcast.110, s32[2048]{0:T(1024)S(1)} %get-tuple-element.292, s32[1024]{0:T(1024)S(1)} %dynamic_slice.32, f32[1,88,2048]{2,1,0:T(8,128)S(1)} %get-tuple-element.278, f32[2048]{0:T(1024)S(1)} %bitcast.117, ...), kind=kOutput, calls=%fused_computation.12.clone.1 | convolution fusion | flops 380125184 | bytes 10039305 | tf_op jit(solution)/shard_map/while/body/eval_jaxpr/hqk,hdk->hdq/dot_general | solution.py:73
  180.0 5.6 %fusion.45 = (f32[2048]{0:T(1024)S(1)}, f32[1024,2048]{1,0:T(8,128)}) fusion(s32[2048]{0:T(1024)S(1)} %get-tuple-element.292, s32[1024]{0:T(1024)S(1)} %dynamic_slice.32, bf16[1,88,2048]{2,1,0:T(8,128)(2,1)S(1)} %get-tuple-element.295, bf16[2,88,16384]{2,1,0:T(8,128)(2,1)} %get-tuple-element.294, s32[]{:T(128)S(6)} %select_n.132), kind=kOutput, calls=%fused_computation.5.clone.1 | convolution fusion | flops 377485312 | bytes 8949764 | tf_op jit(solution)/shard_map/while/body/eval_jaxpr/hdq,hdk->hqk/dot_general | solution.py:65
  185.6 4.7 fusion.47
  190.4 5.4 %fusion.49 = f32[1,88,2048]{2,1,0:T(8,128)S(1)} fusion(f32[1024,2048]{1,0:T(8,128)} %get-tuple-element.259, f32[2048]{0:T(1024)S(1)} %bitcast.110, s32[2048]{0:T(1024)S(1)} %get-tuple-element.292, s32[1024]{0:T(1024)S(1)} %dynamic_slice.32, f32[1,88,2048]{2,1,0:T(8,128)S(1)} %get-tuple-element.278, f32[2048]{0:T(1024)S(1)} %bitcast.117, ...), kind=kOutput, calls=%fused_computation.12.clone.1 | convolution fusion | flops 380125184 | bytes 10039305 | tf_op jit(solution)/shard_map/while/body/eval_jaxpr/hqk,hdk->hdq/dot_general | solution.py:73
  195.8 5.6 %fusion.45 = (f32[2048]{0:T(1024)S(1)}, f32[1024,2048]{1,0:T(8,128)}) fusion(s32[2048]{0:T(1024)S(1)} %get-tuple-element.292, s32[1024]{0:T(1024)S(1)} %dynamic_slice.32, bf16[1,88,2048]{2,1,0:T(8,128)(2,1)S(1)} %get-tuple-element.295, bf16[2,88,16384]{2,1,0:T(8,128)(2,1)} %get-tuple-element.294, s32[]{:T(128)S(6)} %select_n.132), kind=kOutput, calls=%fused_computation.5.clone.1 | convolution fusion | flops 377485312 | bytes 8949764 | tf_op jit(solution)/shard_map/while/body/eval_jaxpr/hdq,hdk->hqk/dot_general | solution.py:65
  206.0 5.9 %fusion.49 = f32[1,88,2048]{2,1,0:T(8,128)S(1)} fusion(f32[1024,2048]{1,0:T(8,128)} %get-tuple-element.259, f32[2048]{0:T(1024)S(1)} %bitcast.110, s32[2048]{0:T(1024)S(1)} %get-tuple-element.292, s32[1024]{0:T(1024)S(1)} %dynamic_slice.32, f32[1,88,2048]{2,1,0:T(8,128)S(1)} %get-tuple-element.278, f32[2048]{0:T(1024)S(1)} %bitcast.117, ...), kind=kOutput, calls=%fused_computation.12.clone.1 | convolution fusion | flops 380125184 | bytes 10039305 | tf_op jit(solution)/shard_map/while/body/eval_jaxpr/hqk,hdk->hdq/dot_general | solution.py:73
  212.0 5.6 %fusion.45 = (f32[2048]{0:T(1024)S(1)}, f32[1024,2048]{1,0:T(8,128)}) fusion(s32[2048]{0:T(1024)S(1)} %get-tuple-element.292, s32[1024]{0:T(1024)S(1)} %dynamic_slice.32, bf16[1,88,2048]{2,1,0:T(8,128)(2,1)S(1)} %get-tuple-element.295, bf16[2,88,16384]{2,1,0:T(8,128)(2,1)} %get-tuple-element.294, s32[]{:T(128)S(6)} %select_n.132), kind=kOutput, calls=%fused_computation.5.clone.1 | convolution fusion | flops 377485312 | bytes 8949764 | tf_op jit(solution)/shard_map/while/body/eval_jaxpr/hdq,hdk->hqk/dot_general | solution.py:65
  217.5 4.7 fusion.47
  222.3 5.4 %fusion.49 = f32[1,88,2048]{2,1,0:T(8,128)S(1)} fusion(f32[1024,2048]{1,0:T(8,128)} %get-tuple-element.259, f32[2048]{0:T(1024)S(1)} %bitcast.110, s32[2048]{0:T(1024)S(1)} %get-tuple-element.292, s32[1024]{0:T(1024)S(1)} %dynamic_slice.32, f32[1,88,2048]{2,1,0:T(8,128)S(1)} %get-tuple-element.278, f32[2048]{0:T(1024)S(1)} %bitcast.117, ...), kind=kOutput, calls=%fused_computation.12.clone.1 | convolution fusion | flops 380125184 | bytes 10039305 | tf_op jit(solution)/shard_map/while/body/eval_jaxpr/hqk,hdk->hdq/dot_general | solution.py:73
  227.8 5.6 %fusion.45 = (f32[2048]{0:T(1024)S(1)}, f32[1024,2048]{1,0:T(8,128)}) fusion(s32[2048]{0:T(1024)S(1)} %get-tuple-element.292, s32[1024]{0:T(1024)S(1)} %dynamic_slice.32, bf16[1,88,2048]{2,1,0:T(8,128)(2,1)S(1)} %get-tuple-element.295, bf16[2,88,16384]{2,1,0:T(8,128)(2,1)} %get-tuple-element.294, s32[]{:T(128)S(6)} %select_n.132), kind=kOutput, calls=%fused_computation.5.clone.1 | convolution fusion | flops 377485312 | bytes 8949764 | tf_op jit(solution)/shard_map/while/body/eval_jaxpr/hdq,hdk->hqk/dot_general | solution.py:65
  233.4 5.9 %fusion.47 = f32[2048]{0:T(1024)S(1)} fusion(f32[1024,2048]{1,0:T(8,128)} %get-tuple-element.259, f32[2048]{0:T(1024)S(1)} %bitcast.109, s32[2048]{0:T(1024)S(1)} %get-tuple-element.292, s32[1024]{0:T(1024)S(1)} %dynamic_slice.32), kind=kLoop, calls=%fused_computation.9.clone.1 | loop fusion | flops 10483712 | bytes 8417280 | tf_op jit(solution)/shard_map/while/body/eval_jaxpr/reduce_sum | solution.py:72
  239.3 5.4 %fusion.49 = f32[1,88,2048]{2,1,0:T(8,128)S(1)} fusion(f32[1024,2048]{1,0:T(8,128)} %get-tuple-element.259, f32[2048]{0:T(1024)S(1)} %bitcast.110, s32[2048]{0:T(1024)S(1)} %get-tuple-element.292, s32[1024]{0:T(1024)S(1)} %dynamic_slice.32, f32[1,88,2048]{2,1,0:T(8,128)S(1)} %get-tuple-element.278, f32[2048]{0:T(1024)S(1)} %bitcast.117, ...), kind=kOutput, calls=%fused_computation.12.clone.1 | convolution fusion | flops 380125184 | bytes 10039305 | tf_op jit(solution)/shard_map/while/body/eval_jaxpr/hqk,hdk->hdq/dot_general | solution.py:73
  244.8 5.6 %fusion.45 = (f32[2048]{0:T(1024)S(1)}, f32[1024,2048]{1,0:T(8,128)}) fusion(s32[2048]{0:T(1024)S(1)} %get-tuple-element.292, s32[1024]{0:T(1024)S(1)} %dynamic_slice.32, bf16[1,88,2048]{2,1,0:T(8,128)(2,1)S(1)} %get-tuple-element.295, bf16[2,88,16384]{2,1,0:T(8,128)(2,1)} %get-tuple-element.294, s32[]{:T(128)S(6)} %select_n.132), kind=kOutput, calls=%fused_computation.5.clone.1 | convolution fusion | flops 377485312 | bytes 8949764 | tf_op jit(solution)/shard_map/while/body/eval_jaxpr/hdq,hdk->hqk/dot_general | solution.py:65
  250.4 4.8 fusion.47
  255.2 5.7 %fusion.49 = f32[1,88,2048]{2,1,0:T(8,128)S(1)} fusion(f32[1024,2048]{1,0:T(8,128)} %get-tuple-element.259, f32[2048]{0:T(1024)S(1)} %bitcast.110, s32[2048]{0:T(1024)S(1)} %get-tuple-element.292, s32[1024]{0:T(1024)S(1)} %dynamic_slice.32, f32[1,88,2048]{2,1,0:T(8,128)S(1)} %get-tuple-element.278, f32[2048]{0:T(1024)S(1)} %bitcast.117, ...), kind=kOutput, calls=%fused_computation.12.clone.1 | convolution fusion | flops 380125184 | bytes 10039305 | tf_op jit(solution)/shard_map/while/body/eval_jaxpr/hqk,hdk->hdq/dot_general | solution.py:73
  261.0 5.6 %fusion.45 = (f32[2048]{0:T(1024)S(1)}, f32[1024,2048]{1,0:T(8,128)}) fusion(s32[2048]{0:T(1024)S(1)} %get-tuple-element.292, s32[1024]{0:T(1024)S(1)} %dynamic_slice.32, bf16[1,88,2048]{2,1,0:T(8,128)(2,1)S(1)} %get-tuple-element.295, bf16[2,88,16384]{2,1,0:T(8,128)(2,1)} %get-tuple-element.294, s32[]{:T(128)S(6)} %select_n.132), kind=kOutput, calls=%fused_computation.5.clone.1 | convolution fusion | flops 377485312 | bytes 8949764 | tf_op jit(solution)/shard_map/while/body/eval_jaxpr/hdq,hdk->hqk/dot_general | solution.py:65
  266.6 4.8 fusion.47
  271.4 5.7 %fusion.49 = f32[1,88,2048]{2,1,0:T(8,128)S(1)} fusion(f32[1024,2048]{1,0:T(8,128)} %get-tuple-element.259, f32[2048]{0:T(1024)S(1)} %bitcast.110, s32[2048]{0:T(1024)S(1)} %get-tuple-element.292, s32[1024]{0:T(1024)S(1)} %dynamic_slice.32, f32[1,88,2048]{2,1,0:T(8,128)S(1)} %get-tuple-element.278, f32[2048]{0:T(1024)S(1)} %bitcast.117, ...), kind=kOutput, calls=%fused_computation.12.clone.1 | convolution fusion | flops 380125184 | bytes 10039305 | tf_op jit(solution)/shard_map/while/body/eval_jaxpr/hqk,hdk->hdq/dot_general | solution.py:73
  277.1 5.6 %fusion.45 = (f32[2048]{0:T(1024)S(1)}, f32[1024,2048]{1,0:T(8,128)}) fusion(s32[2048]{0:T(1024)S(1)} %get-tuple-element.292, s32[1024]{0:T(1024)S(1)} %dynamic_slice.32, bf16[1,88,2048]{2,1,0:T(8,128)(2,1)S(1)} %get-tuple-element.295, bf16[2,88,16384]{2,1,0:T(8,128)(2,1)} %get-tuple-element.294, s32[]{:T(128)S(6)} %select_n.132), kind=kOutput, calls=%fused_computation.5.clone.1 | convolution fusion | flops 377485312 | bytes 8949764 | tf_op jit(solution)/shard_map/while/body/eval_jaxpr/hdq,hdk->hqk/dot_general | solution.py:65
  287.4 5.4 %fusion.49 = f32[1,88,2048]{2,1,0:T(8,128)S(1)} fusion(f32[1024,2048]{1,0:T(8,128)} %get-tuple-element.259, f32[2048]{0:T(1024)S(1)} %bitcast.110, s32[2048]{0:T(1024)S(1)} %get-tuple-element.292, s32[1024]{0:T(1024)S(1)} %dynamic_slice.32, f32[1,88,2048]{2,1,0:T(8,128)S(1)} %get-tuple-element.278, f32[2048]{0:T(1024)S(1)} %bitcast.117, ...), kind=kOutput, calls=%fused_computation.12.clone.1 | convolution fusion | flops 380125184 | bytes 10039305 | tf_op jit(solution)/shard_map/while/body/eval_jaxpr/hqk,hdk->hdq/dot_general | solution.py:73
  292.9 5.6 %fusion.45 = (f32[2048]{0:T(1024)S(1)}, f32[1024,2048]{1,0:T(8,128)}) fusion(s32[2048]{0:T(1024)S(1)} %get-tuple-element.292, s32[1024]{0:T(1024)S(1)} %dynamic_slice.32, bf16[1,88,2048]{2,1,0:T(8,128)(2,1)S(1)} %get-tuple-element.295, bf16[2,88,16384]{2,1,0:T(8,128)(2,1)} %get-tuple-element.294, s32[]{:T(128)S(6)} %select_n.132), kind=kOutput, calls=%fused_computation.5.clone.1 | convolution fusion | flops 377485312 | bytes 8949764 | tf_op jit(solution)/shard_map/while/body/eval_jaxpr/hdq,hdk->hqk/dot_general | solution.py:65
  303.1 5.4 %fusion.49 = f32[1,88,2048]{2,1,0:T(8,128)S(1)} fusion(f32[1024,2048]{1,0:T(8,128)} %get-tuple-element.259, f32[2048]{0:T(1024)S(1)} %bitcast.110, s32[2048]{0:T(1024)S(1)} %get-tuple-element.292, s32[1024]{0:T(1024)S(1)} %dynamic_slice.32, f32[1,88,2048]{2,1,0:T(8,128)S(1)} %get-tuple-element.278, f32[2048]{0:T(1024)S(1)} %bitcast.117, ...), kind=kOutput, calls=%fused_computation.12.clone.1 | convolution fusion | flops 380125184 | bytes 10039305 | tf_op jit(solution)/shard_map/while/body/eval_jaxpr/hqk,hdk->hdq/dot_general | solution.py:73
  308.6 5.6 %fusion.45 = (f32[2048]{0:T(1024)S(1)}, f32[1024,2048]{1,0:T(8,128)}) fusion(s32[2048]{0:T(1024)S(1)} %get-tuple-element.292, s32[1024]{0:T(1024)S(1)} %dynamic_slice.32, bf16[1,88,2048]{2,1,0:T(8,128)(2,1)S(1)} %get-tuple-element.295, bf16[2,88,16384]{2,1,0:T(8,128)(2,1)} %get-tuple-element.294, s32[]{:T(128)S(6)} %select_n.132), kind=kOutput, calls=%fused_computation.5.clone.1 | convolution fusion | flops 377485312 | bytes 8949764 | tf_op jit(solution)/shard_map/while/body/eval_jaxpr/hdq,hdk->hqk/dot_general | solution.py:65
  318.8 5.4 %fusion.49 = f32[1,88,2048]{2,1,0:T(8,128)S(1)} fusion(f32[1024,2048]{1,0:T(8,128)} %get-tuple-element.259, f32[2048]{0:T(1024)S(1)} %bitcast.110, s32[2048]{0:T(1024)S(1)} %get-tuple-element.292, s32[1024]{0:T(1024)S(1)} %dynamic_slice.32, f32[1,88,2048]{2,1,0:T(8,128)S(1)} %get-tuple-element.278, f32[2048]{0:T(1024)S(1)} %bitcast.117, ...), kind=kOutput, calls=%fused_computation.12.clone.1 | convolution fusion | flops 380125184 | bytes 10039305 | tf_op jit(solution)/shard_map/while/body/eval_jaxpr/hqk,hdk->hdq/dot_general | solution.py:73
  324.2 5.6 %fusion.45 = (f32[2048]{0:T(1024)S(1)}, f32[1024,2048]{1,0:T(8,128)}) fusion(s32[2048]{0:T(1024)S(1)} %get-tuple-element.292, s32[1024]{0:T(1024)S(1)} %dynamic_slice.32, bf16[1,88,2048]{2,1,0:T(8,128)(2,1)S(1)} %get-tuple-element.295, bf16[2,88,16384]{2,1,0:T(8,128)(2,1)} %get-tuple-element.294, s32[]{:T(128)S(6)} %select_n.132), kind=kOutput, calls=%fused_computation.5.clone.1 | convolution fusion | flops 377485312 | bytes 8949764 | tf_op jit(solution)/shard_map/while/body/eval_jaxpr/hdq,hdk->hqk/dot_general | solution.py:65
  334.4 5.4 %fusion.49 = f32[1,88,2048]{2,1,0:T(8,128)S(1)} fusion(f32[1024,2048]{1,0:T(8,128)} %get-tuple-element.259, f32[2048]{0:T(1024)S(1)} %bitcast.110, s32[2048]{0:T(1024)S(1)} %get-tuple-element.292, s32[1024]{0:T(1024)S(1)} %dynamic_slice.32, f32[1,88,2048]{2,1,0:T(8,128)S(1)} %get-tuple-element.278, f32[2048]{0:T(1024)S(1)} %bitcast.117, ...), kind=kOutput, calls=%fused_computation.12.clone.1 | convolution fusion | flops 380125184 | bytes 10039305 | tf_op jit(solution)/shard_map/while/body/eval_jaxpr/hqk,hdk->hdq/dot_general | solution.py:73
  339.9 5.6 %fusion.45 = (f32[2048]{0:T(1024)S(1)}, f32[1024,2048]{1,0:T(8,128)}) fusion(s32[2048]{0:T(1024)S(1)} %get-tuple-element.292, s32[1024]{0:T(1024)S(1)} %dynamic_slice.32, bf16[1,88,2048]{2,1,0:T(8,128)(2,1)S(1)} %get-tuple-element.295, bf16[2,88,16384]{2,1,0:T(8,128)(2,1)} %get-tuple-element.294, s32[]{:T(128)S(6)} %select_n.132), kind=kOutput, calls=%fused_computation.5.clone.1 | convolution fusion | flops 377485312 | bytes 8949764 | tf_op jit(solution)/shard_map/while/body/eval_jaxpr/hdq,hdk->hqk/dot_general | solution.py:65
  350.1 5.4 %fusion.49 = f32[1,88,2048]{2,1,0:T(8,128)S(1)} fusion(f32[1024,2048]{1,0:T(8,128)} %get-tuple-element.259, f32[2048]{0:T(1024)S(1)} %bitcast.110, s32[2048]{0:T(1024)S(1)} %get-tuple-element.292, s32[1024]{0:T(1024)S(1)} %dynamic_slice.32, f32[1,88,2048]{2,1,0:T(8,128)S(1)} %get-tuple-element.278, f32[2048]{0:T(1024)S(1)} %bitcast.117, ...), kind=kOutput, calls=%fused_computation.12.clone.1 | convolution fusion | flops 380125184 | bytes 10039305 | tf_op jit(solution)/shard_map/while/body/eval_jaxpr/hqk,hdk->hdq/dot_general | solution.py:73
  355.6 5.6 %fusion.45 = (f32[2048]{0:T(1024)S(1)}, f32[1024,2048]{1,0:T(8,128)}) fusion(s32[2048]{0:T(1024)S(1)} %get-tuple-element.292, s32[1024]{0:T(1024)S(1)} %dynamic_slice.32, bf16[1,88,2048]{2,1,0:T(8,128)(2,1)S(1)} %get-tuple-element.295, bf16[2,88,16384]{2,1,0:T(8,128)(2,1)} %get-tuple-element.294, s32[]{:T(128)S(6)} %select_n.132), kind=kOutput, calls=%fused_computation.5.clone.1 | convolution fusion | flops 377485312 | bytes 8949764 | tf_op jit(solution)/shard_map/while/body/eval_jaxpr/hdq,hdk->hqk/dot_general | solution.py:65
  365.8 5.4 %fusion.49 = f32[1,88,2048]{2,1,0:T(8,128)S(1)} fusion(f32[1024,2048]{1,0:T(8,128)} %get-tuple-element.259, f32[2048]{0:T(1024)S(1)} %bitcast.110, s32[2048]{0:T(1024)S(1)} %get-tuple-element.292, s32[1024]{0:T(1024)S(1)} %dynamic_slice.32, f32[1,88,2048]{2,1,0:T(8,128)S(1)} %get-tuple-element.278, f32[2048]{0:T(1024)S(1)} %bitcast.117, ...), kind=kOutput, calls=%fused_computation.12.clone.1 | convolution fusion | flops 380125184 | bytes 10039305 | tf_op jit(solution)/shard_map/while/body/eval_jaxpr/hqk,hdk->hdq/dot_general | solution.py:73
  371.2 5.6 %fusion.45 = (f32[2048]{0:T(1024)S(1)}, f32[1024,2048]{1,0:T(8,128)}) fusion(s32[2048]{0:T(1024)S(1)} %get-tuple-element.292, s32[1024]{0:T(1024)S(1)} %dynamic_slice.32, bf16[1,88,2048]{2,1,0:T(8,128)(2,1)S(1)} %get-tuple-element.295, bf16[2,88,16384]{2,1,0:T(8,128)(2,1)} %get-tuple-element.294, s32[]{:T(128)S(6)} %select_n.132), kind=kOutput, calls=%fused_computation.5.clone.1 | convolution fusion | flops 377485312 | bytes 8949764 | tf_op jit(solution)/shard_map/while/body/eval_jaxpr/hdq,hdk->hqk/dot_general | solution.py:65
  381.4 5.4 %fusion.49 = f32[1,88,2048]{2,1,0:T(8,128)S(1)} fusion(f32[1024,2048]{1,0:T(8,128)} %get-tuple-element.259, f32[2048]{0:T(1024)S(1)} %bitcast.110, s32[2048]{0:T(1024)S(1)} %get-tuple-element.292, s32[1024]{0:T(1024)S(1)} %dynamic_slice.32, f32[1,88,2048]{2,1,0:T(8,128)S(1)} %get-tuple-element.278, f32[2048]{0:T(1024)S(1)} %bitcast.117, ...), kind=kOutput, calls=%fused_computation.12.clone.1 | convolution fusion | flops 380125184 | bytes 10039305 | tf_op jit(solution)/shard_map/while/body/eval_jaxpr/hqk,hdk->hdq/dot_general | solution.py:73
  386.9 5.6 %fusion.45 = (f32[2048]{0:T(1024)S(1)}, f32[1024,2048]{1,0:T(8,128)}) fusion(s32[2048]{0:T(1024)S(1)} %get-tuple-element.292, s32[1024]{0:T(1024)S(1)} %dynamic_slice.32, bf16[1,88,2048]{2,1,0:T(8,128)(2,1)S(1)} %get-tuple-element.295, bf16[2,88,16384]{2,1,0:T(8,128)(2,1)} %get-tuple-element.294, s32[]{:T(128)S(6)} %select_n.132), kind=kOutput, calls=%fused_computation.5.clone.1 | convolution fusion | flops 377485312 | bytes 8949764 | tf_op jit(solution)/shard_map/while/body/eval_jaxpr/hdq,hdk->hqk/dot_general | solution.py:65
  397.1 5.4 %fusion.49 = f32[1,88,2048]{2,1,0:T(8,128)S(1)} fusion(f32[1024,2048]{1,0:T(8,128)} %get-tuple-element.259, f32[2048]{0:T(1024)S(1)} %bitcast.110, s32[2048]{0:T(1024)S(1)} %get-tuple-element.292, s32[1024]{0:T(1024)S(1)} %dynamic_slice.32, f32[1,88,2048]{2,1,0:T(8,128)S(1)} %get-tuple-element.278, f32[2048]{0:T(1024)S(1)} %bitcast.117, ...), kind=kOutput, calls=%fused_computation.12.clone.1 | convolution fusion | flops 380125184 | bytes 10039305 | tf_op jit(solution)/shard_map/while/body/eval_jaxpr/hqk,hdk->hdq/dot_general | solution.py:73
  403.5 6.1 %all-to-all-start = ((bf16[88,16,128]{2,0,1:T(8,128)(2,1)}), bf16[88,16,128]{2,0,1:T(8,128)(2,1)S(1)}, u32[]{:S(2)}, u32[]{:S(2)}) async-start(bf16[88,16,128]{2,0,1:T(8,128)(2,1)} %copy.32), calls=%async_computation | async-start | bytes 720896 | tf_op jit(solution)/shard_map/all_to_all | solution.py:102
  409.7 7.7 %convert_element_type.50 = f32[1408,2048]{0,1:T(8,128)} convert(bf16[1408,2048]{0,1:T(8,128)(2,1)} %copy.28) | non-fusion elementwise | flops 2883584 | bytes 17301504 | tf_op jit(solution)/shard_map/convert_element_type | solution.py:33
  423.1 8.8 %fusion.23 = bf16[32,1408]{1,0:T(8,128)(2,1)} fusion(bf16[4,1408,1408]{2,1,0:T(8,128)(2,1)} %all-gather.12.cloned.1.call-done, bf16[1408,32,4]{0,2,1:T(4,128)(2,1)S(1)} %reshape.212), kind=kOutput, calls=%fused_computation.36 | convolution fusion | flops 507555840 | bytes 16310272 | tf_op jit(solution)/shard_map/fgi,ifd->gd/dot_general | solution.py:118
  433.3 41.2 %all-gather.14.cloned.1.call-done = bf16[512,1408]{1,0:T(8,128)(2,1)} async-done(((bf16[32,1408]{1,0:T(8,128)(2,1)}), bf16[512,1408]{1,0:T(8,128)(2,1)}) %all-gather.14.cloned.1.call-update) | async-done | bytes 1441808 | tf_op jit(solution)/shard_map/all_gather | solution.py:119
  (132 shorter events, 86.3 us)
Async XLA Ops:
  6.5 86.1 %copy-start = (bf16[2,88,1408]{2,1,0:T(8,128)(2,1)S(1)}, bf16[2,88,1408]{2,1,0:T(8,128)(2,1)}, u32[]{:S(2)}) copy-start(bf16[2,88,1408]{2,1,0:T(8,128)(2,1)} %param.16) | copy-start | bytes 1486852
  6.5 64.2 %all-gather.6.cloned.1.call-start = ((), (), s32[]{:S(2)}) async-start(), calls=%async_computation.1 | async-start | bytes 6127616 | tf_op jit(solution)/shard_map/all_gather | solution.py:31
  7.3 134.4 %all-gather.8.cloned.1.call-start = ((), (), s32[]{:S(2)}) async-start(), calls=%async_computation.2 | async-start | bytes 6782976 | tf_op jit(solution)/shard_map/all_gather | solution.py:56
  79.1 4.5 copy-start.2
  87.6 15.2 %copy-start.4 = (bf16[88,1408]{1,0:T(8,128)(2,1)S(1)}, bf16[88,1408]{1,0:T(8,128)(2,1)}, u32[]{:S(2)}) copy-start(bf16[88,1408]{1,0:T(8,128)(2,1)} %param.15) | copy-start | bytes 743428
  101.8 315.6 %all-gather.10.cloned.1.call-start = ((), (), s32[]{:S(2)}) async-start(), calls=%async_computation.3 | async-start | bytes 4212736 | tf_op jit(solution)/shard_map/all_gather | solution.py:32
  102.5 320.5 %all-gather.12.cloned.1.call-start = ((), (), s32[]{:S(2)}) async-start(), calls=%async_computation.4 | async-start | bytes 16850944 | tf_op jit(solution)/shard_map/all_gather | solution.py:116
  102.8 45.7 %copy-start.3 = (s32[2048]{0:T(1024)S(1)}, s32[2048]{0:T(1024)}, u32[]{:S(2)}) copy-start(s32[2048]{0:T(1024)} %param.19) | copy-start | bytes 24580
  148.5 261.2 %copy-start.5 = (bf16[1408]{0:T(1024)(128)(2,1)S(1)}, bf16[1408]{0:T(1024)(128)(2,1)}, u32[]{:S(2)}) copy-start(bf16[1408]{0:T(1024)(128)(2,1)} %param.21) | copy-start | bytes 8452
  403.5 16.0 %all-to-all-start = ((bf16[88,16,128]{2,0,1:T(8,128)(2,1)}), bf16[88,16,128]{2,0,1:T(8,128)(2,1)S(1)}, u32[]{:S(2)}, u32[]{:S(2)}) async-start(bf16[88,16,128]{2,0,1:T(8,128)(2,1)} %copy.32), calls=%async_computation | async-start | bytes 720896 | tf_op jit(solution)/shard_map/all_to_all | solution.py:102
  409.6 64.9 %all-gather.14.cloned.1.call-start = ((), (), s32[]{:S(2)}) async-start(), calls=%async_computation.5 | async-start | bytes 1531904 | tf_op jit(solution)/shard_map/all_gather | solution.py:119
  422.9 54.9 %copy-start.1 = (bf16[2,88,1408]{2,1,0:T(8,128)(2,1)S(1)}, bf16[2,88,1408]{2,1,0:T(8,128)(2,1)}, u32[]{:S(2)}) copy-start(bf16[2,88,1408]{2,1,0:T(8,128)(2,1)} %param.16) | copy-start | bytes 1486852
Sparse Core Ops, SparseCore 0:
  9.5 61.1 all-gather.5
  101.9 39.7 all-gather.7
  143.8 50.4 all-gather.9
  196.4 106.0 all-gather.11
  432.0 42.4 all-gather.13
where the time goes:
time: 486 us; the launch traced here: 484 us
  matrix products  194 us (40%)
  waiting for transfers between devices  137 us (28%)
  other arithmetic  99.7 us (21%)
  local copies, waits for them, and re-layouts  33 us (7%)
  between operations  13.4 us (3%)
  starting transfers between devices  6.4 us (1%)
    dot_general x16, matrix products, take_block(): jnp.einsum('hdq,hdk->hqk', query_heads, key_block, preferred_element_type...  89.1 us
    dot_general x16, matrix products, take_block(): jnp.einsum('hqk,hdk->hdq', weights_exp.astype(jnp.bfloat16), value_block,...  87.5 us
    reduce_sum x16, other arithmetic, take_block(): running_sum = running_sum * factor + jnp.sum(weights_exp, axis=2)  75.4 us
    all_gather x1, waiting for transfers between devices, on_device(): full_rows = lax.all_gather(hidden, 'col', axis=0, tiled=True)  58.2 us
    all_gather x1, waiting for transfers between devices, on_device(): lax.all_gather(merged_here.astype(jnp.bfloat16), 'col', axis=0, tiled=True)  41.2 us
    all_gather x1, waiting for transfers between devices, on_device(): pair_all = lax.all_gather(pair_local, 'row', axis=1, tiled=True)  34.2 us
  transfers between devices with their start and end apart: 6, of which 4 were waited for; matrix products, arithmetic and copies ran while one was open for 58% of the time, Pallas kernels for 0%

commit v1 on v0

--- a/solution.py
+++ b/solution.py
@@ -116,7 +116,12 @@
     merge_full = lax.all_gather(merge_weight, "col", axis=1, tiled=True)
     grouped = merger_chunk.reshape(model_width, chunk // 4, 4)
     merged_here = jnp.einsum("fgi,ifd->gd", grouped, merge_full, preferred_element_type=jnp.float32)
-    merged_all = lax.all_gather(merged_here.astype(jnp.bfloat16), "col", axis=0, tiled=True)
+    merged_all = jnp.concatenate(
+        lax.all_to_all(
+            jnp.stack([merged_here.astype(jnp.bfloat16)] * lax.axis_size("col")), "col", 0, 0
+        ),
+        axis=0,
+    )
     wanted_rows = lax.dynamic_index_in_dim(requests[0], col_index, 0, keepdims=False)
     is_valid = wanted_rows >= 0
     safe_index = jnp.where(is_valid, wanted_rows, 0)

time: 486 us -> 469 us (0.965)
  waiting for transfers between devices: 137 us -> 117 us
  starting transfers between devices: 6.4 us -> 11.3 us
    all_gather x1 -> x0, waiting for transfers between devices: 41.2 us -> none  [on_device(): lax.all_gather(merged_here.astype(jnp.bfloat16), 'col', axis=0, tiled=True)]
    all_to_all x0 -> x1, waiting for transfers between devices: none -> 20.5 us  [on_device(): lax.all_to_all(jnp.stack([merged_here.astype(jnp.bfloat16)] * lax.axis_si...]
    all_to_all x0 -> x1, starting transfers between devices: none -> 4.97 us  [on_device(): lax.all_to_all(jnp.stack([merged_here.astype(jnp.bfloat16)] * lax.axis_si...]
  transfers between devices with their start and end apart: 6 -> 6, of which waited for: 4 -> 4; matrix products, arithmetic and copies ran while one was open for 58% -> 61% of each run, Pallas kernels for 0% -> 0%
where the time goes in v1:
time: 469 us; the launch traced here: 468 us
  matrix products  193 us (41%)
  waiting for transfers between devices  117 us (25%)
  other arithmetic  99.7 us (21%)
  local copies, waits for them, and re-layouts  32.5 us (7%)
  between operations  13.4 us (3%)
  starting transfers between devices  11.3 us (2%)
    dot_general x16, matrix products, take_block(): jnp.einsum('hdq,hdk->hqk', query_heads, key_block, preferred_element_type...  89.2 us
    dot_general x16, matrix products, take_block(): jnp.einsum('hqk,hdk->hdq', weights_exp.astype(jnp.bfloat16), value_block,...  87.5 us
    reduce_sum x16, other arithmetic, take_block(): running_sum = running_sum * factor + jnp.sum(weights_exp, axis=2)  75.4 us
    all_gather x1, waiting for transfers between devices, on_device(): full_rows = lax.all_gather(hidden, 'col', axis=0, tiled=True)  58.2 us
    all_gather x1, waiting for transfers between devices, on_device(): pair_all = lax.all_gather(pair_local, 'row', axis=1, tiled=True)  34.2 us
    all_to_all x1, waiting for transfers between devices, on_device(): lax.all_to_all(jnp.stack([merged_here.astype(jnp.bfloat16)] * lax.axis_si...  20.5 us
  transfers between devices with their start and end apart: 6, of which 4 were waited for; matrix products, arithmetic and copies ran while one was open for 61% of the time, Pallas kernels for 0%

profile of v1, /device:TPU:0, one launch (start us, length us, event | category | flops | bytes accessed | tf_op | source)
XLA Modules:
  0.0 467.5 jit_solution(7236269267447843662)
XLA Ops:
  12.5 58.2 %all-gather.5.cloned.1.call-done = bf16[1408,2048]{1,0:T(8,128)(2,1)} async-done(((bf16[88,2048]{1,0:T(8,128)(2,1)}), bf16[1408,2048]{1,0:T(8,128)(2,1)}) %all-gather.5.cloned.1.call-update) | async-done | bytes 5767184 | tf_op jit(solution)/shard_map/all_gather | solution.py:31
  70.7 8.3 %copy.28 = bf16[1408,2048]{0,1:T(8,128)(2,1)} copy(bf16[1408,2048]{1,0:T(8,128)(2,1)} %all-gather.5.cloned.1.call-done) | data formatting | bytes 11534336 | tf_op jit(solution)/shard_map/all_gather | solution.py:31
  87.6 5.0 %gather_fusion = bf16[200,1408]{1,0:T(8,128)(2,1)S(1)} fusion(bf16[1408,2048]{0,1:T(8,128)(2,1)} %multiply_convert_fusion, s32[1024]{0:T(1024)S(1)} %pad_clamp_fusion.1), kind=kCustom, calls=%fused_computation | custom fusion | bytes 1127200 | tf_op jit(solution)/shard_map/jit(_take)/gather | solution.py:43
  93.2 6.9 %scatter_fusion = bf16[2,88,2048]{1,0,2:T(2,128)(2,1)S(1)} fusion(bf16[2,88,2048]{1,0,2:T(2,128)(2,1)S(1)} %copy.30, s32[200]{0:T(256)S(1)} %bitcast.124, bf16[200,2,88]{2,1,0:T(2,128)(2,1)S(1)} %bitcast.117), kind=kCustom, calls=%fused_computation.2 | custom fusion | bytes 212000 | tf_op jit(solution)/shard_map/scatter | solution.py:50
  107.5 34.2 %all-gather.7.cloned.1.call-done = bf16[177,16384]{1,0:T(8,128)(2,1)} async-done(((bf16[177,2048]{1,0:T(8,128)(2,1)}), bf16[177,16384]{1,0:T(8,128)(2,1)}) %all-gather.7.cloned.1.call-update) | async-done | bytes 5799952 | tf_op jit(solution)/shard_map/all_gather | solution.py:56
  141.7 5.8 %slice.29 = bf16[176,16384]{1,0:T(8,128)(2,1)} slice(bf16[177,16384]{1,0:T(8,128)(2,1)} %all-gather.7.cloned.1.call-done), slice={[0:176], [0:16384]} | slice | bytes 11534336 | tf_op jit(solution)/shard_map/slice | solution.py:57
  148.5 254.0 %while.18 = (s32[]{:T(128)}, f32[1,2048]{1,0:T(1,128)S(1)}, f32[1,2048]{1,0:T(1,128)S(1)}, f32[1,88,2048]{2,1,0:T(8,128)S(1)}, s32[2048]{0:T(1024)S(1)}, /*index...) while((s32[]{:T(128)}, f32[1,2048]{1,0:T(1,128)S(1)}, ...), condition=%wide.region_6.7_spmd.clone, body=%wide.region_3.0_spmd.clone.sunk | while | flops 768108544 | bytes 27504848 | solution.py:97
  148.6 5.6 %fusion.45 = (f32[2048]{0:T(1024)S(1)}, f32[1024,2048]{1,0:T(8,128)}) fusion(s32[2048]{0:T(1024)S(1)} %get-tuple-element.292, s32[1024]{0:T(1024)S(1)} %dynamic_slice.32, bf16[1,88,2048]{2,1,0:T(8,128)(2,1)S(1)} %get-tuple-element.295, bf16[2,88,16384]{2,1,0:T(8,128)(2,1)} %get-tuple-element.294, s32[]{:T(128)S(6)} %select_n.132), kind=kOutput, calls=%fused_computation.5.clone.1 | convolution fusion | flops 377485312 | bytes 8949764 | tf_op jit(solution)/shard_map/while/body/eval_jaxpr/hdq,hdk->hqk/dot_general | solution.py:65
  158.8 5.5 %fusion.49 = f32[1,88,2048]{2,1,0:T(8,128)S(1)} fusion(f32[1024,2048]{1,0:T(8,128)} %get-tuple-element.259, f32[2048]{0:T(1024)S(1)} %bitcast.112, s32[2048]{0:T(1024)S(1)} %get-tuple-element.292, s32[1024]{0:T(1024)S(1)} %dynamic_slice.32, f32[1,88,2048]{2,1,0:T(8,128)S(1)} %get-tuple-element.278, f32[2048]{0:T(1024)S(1)} %bitcast.119, ...), kind=kOutput, calls=%fused_computation.12.clone.1 | convolution fusion | flops 380125184 | bytes 10039305 | tf_op jit(solution)/shard_map/while/body/eval_jaxpr/hqk,hdk->hdq/dot_general | solution.py:73
  164.3 5.6 %fusion.45 = (f32[2048]{0:T(1024)S(1)}, f32[1024,2048]{1,0:T(8,128)}) fusion(s32[2048]{0:T(1024)S(1)} %get-tuple-element.292, s32[1024]{0:T(1024)S(1)} %dynamic_slice.32, bf16[1,88,2048]{2,1,0:T(8,128)(2,1)S(1)} %get-tuple-element.295, bf16[2,88,16384]{2,1,0:T(8,128)(2,1)} %get-tuple-element.294, s32[]{:T(128)S(6)} %select_n.132), kind=kOutput, calls=%fused_computation.5.clone.1 | convolution fusion | flops 377485312 | bytes 8949764 | tf_op jit(solution)/shard_map/while/body/eval_jaxpr/hdq,hdk->hqk/dot_general | solution.py:65
  174.5 5.4 %fusion.49 = f32[1,88,2048]{2,1,0:T(8,128)S(1)} fusion(f32[1024,2048]{1,0:T(8,128)} %get-tuple-element.259, f32[2048]{0:T(1024)S(1)} %bitcast.112, s32[2048]{0:T(1024)S(1)} %get-tuple-element.292, s32[1024]{0:T(1024)S(1)} %dynamic_slice.32, f32[1,88,2048]{2,1,0:T(8,128)S(1)} %get-tuple-element.278, f32[2048]{0:T(1024)S(1)} %bitcast.119, ...), kind=kOutput, calls=%fused_computation.12.clone.1 | convolution fusion | flops 380125184 | bytes 10039305 | tf_op jit(solution)/shard_map/while/body/eval_jaxpr/hqk,hdk->hdq/dot_general | solution.py:73
  180.0 5.6 %fusion.45 = (f32[2048]{0:T(1024)S(1)}, f32[1024,2048]{1,0:T(8,128)}) fusion(s32[2048]{0:T(1024)S(1)} %get-tuple-element.292, s32[1024]{0:T(1024)S(1)} %dynamic_slice.32, bf16[1,88,2048]{2,1,0:T(8,128)(2,1)S(1)} %get-tuple-element.295, bf16[2,88,16384]{2,1,0:T(8,128)(2,1)} %get-tuple-element.294, s32[]{:T(128)S(6)} %select_n.132), kind=kOutput, calls=%fused_computation.5.clone.1 | convolution fusion | flops 377485312 | bytes 8949764 | tf_op jit(solution)/shard_map/while/body/eval_jaxpr/hdq,hdk->hqk/dot_general | solution.py:65
  190.4 5.4 %fusion.49 = f32[1,88,2048]{2,1,0:T(8,128)S(1)} fusion(f32[1024,2048]{1,0:T(8,128)} %get-tuple-element.259, f32[2048]{0:T(1024)S(1)} %bitcast.112, s32[2048]{0:T(1024)S(1)} %get-tuple-element.292, s32[1024]{0:T(1024)S(1)} %dynamic_slice.32, f32[1,88,2048]{2,1,0:T(8,128)S(1)} %get-tuple-element.278, f32[2048]{0:T(1024)S(1)} %bitcast.119, ...), kind=kOutput, calls=%fused_computation.12.clone.1 | convolution fusion | flops 380125184 | bytes 10039305 | tf_op jit(solution)/shard_map/while/body/eval_jaxpr/hqk,hdk->hdq/dot_general | solution.py:73
  195.8 5.6 %fusion.45 = (f32[2048]{0:T(1024)S(1)}, f32[1024,2048]{1,0:T(8,128)}) fusion(s32[2048]{0:T(1024)S(1)} %get-tuple-element.292, s32[1024]{0:T(1024)S(1)} %dynamic_slice.32, bf16[1,88,2048]{2,1,0:T(8,128)(2,1)S(1)} %get-tuple-element.295, bf16[2,88,16384]{2,1,0:T(8,128)(2,1)} %get-tuple-element.294, s32[]{:T(128)S(6)} %select_n.132), kind=kOutput, calls=%fused_computation.5.clone.1 | convolution fusion | flops 377485312 | bytes 8949764 | tf_op jit(solution)/shard_map/while/body/eval_jaxpr/hdq,hdk->hqk/dot_general | solution.py:65
  206.1 5.9 %fusion.49 = f32[1,88,2048]{2,1,0:T(8,128)S(1)} fusion(f32[1024,2048]{1,0:T(8,128)} %get-tuple-element.259, f32[2048]{0:T(1024)S(1)} %bitcast.112, s32[2048]{0:T(1024)S(1)} %get-tuple-element.292, s32[1024]{0:T(1024)S(1)} %dynamic_slice.32, f32[1,88,2048]{2,1,0:T(8,128)S(1)} %get-tuple-element.278, f32[2048]{0:T(1024)S(1)} %bitcast.119, ...), kind=kOutput, calls=%fused_computation.12.clone.1 | convolution fusion | flops 380125184 | bytes 10039305 | tf_op jit(solution)/shard_map/while/body/eval_jaxpr/hqk,hdk->hdq/dot_general | solution.py:73
  212.0 5.6 %fusion.45 = (f32[2048]{0:T(1024)S(1)}, f32[1024,2048]{1,0:T(8,128)}) fusion(s32[2048]{0:T(1024)S(1)} %get-tuple-element.292, s32[1024]{0:T(1024)S(1)} %dynamic_slice.32, bf16[1,88,2048]{2,1,0:T(8,128)(2,1)S(1)} %get-tuple-element.295, bf16[2,88,16384]{2,1,0:T(8,128)(2,1)} %get-tuple-element.294, s32[]{:T(128)S(6)} %select_n.132), kind=kOutput, calls=%fused_computation.5.clone.1 | convolution fusion | flops 377485312 | bytes 8949764 | tf_op jit(solution)/shard_map/while/body/eval_jaxpr/hdq,hdk->hqk/dot_general | solution.py:65
  217.6 4.7 %fusion.47 = f32[2048]{0:T(1024)S(1)} fusion(f32[1024,2048]{1,0:T(8,128)} %get-tuple-element.259, f32[2048]{0:T(1024)S(1)} %bitcast.111, s32[2048]{0:T(1024)S(1)} %get-tuple-element.292, s32[1024]{0:T(1024)S(1)} %dynamic_slice.32), kind=kLoop, calls=%fused_computation.9.clone.1 | loop fusion | flops 10483712 | bytes 8417280 | tf_op jit(solution)/shard_map/while/body/eval_jaxpr/reduce_sum | solution.py:72
  222.4 5.4 %fusion.49 = f32[1,88,2048]{2,1,0:T(8,128)S(1)} fusion(f32[1024,2048]{1,0:T(8,128)} %get-tuple-element.259, f32[2048]{0:T(1024)S(1)} %bitcast.112, s32[2048]{0:T(1024)S(1)} %get-tuple-element.292, s32[1024]{0:T(1024)S(1)} %dynamic_slice.32, f32[1,88,2048]{2,1,0:T(8,128)S(1)} %get-tuple-element.278, f32[2048]{0:T(1024)S(1)} %bitcast.119, ...), kind=kOutput, calls=%fused_computation.12.clone.1 | convolution fusion | flops 380125184 | bytes 10039305 | tf_op jit(solution)/shard_map/while/body/eval_jaxpr/hqk,hdk->hdq/dot_general | solution.py:73
  227.8 5.6 %fusion.45 = (f32[2048]{0:T(1024)S(1)}, f32[1024,2048]{1,0:T(8,128)}) fusion(s32[2048]{0:T(1024)S(1)} %get-tuple-element.292, s32[1024]{0:T(1024)S(1)} %dynamic_slice.32, bf16[1,88,2048]{2,1,0:T(8,128)(2,1)S(1)} %get-tuple-element.295, bf16[2,88,16384]{2,1,0:T(8,128)(2,1)} %get-tuple-element.294, s32[]{:T(128)S(6)} %select_n.132), kind=kOutput, calls=%fused_computation.5.clone.1 | convolution fusion | flops 377485312 | bytes 8949764 | tf_op jit(solution)/shard_map/while/body/eval_jaxpr/hdq,hdk->hqk/dot_general | solution.py:65
  233.4 5.9 %fusion.47 = f32[2048]{0:T(1024)S(1)} fusion(f32[1024,2048]{1,0:T(8,128)} %get-tuple-element.259, f32[2048]{0:T(1024)S(1)} %bitcast.111, s32[2048]{0:T(1024)S(1)} %get-tuple-element.292, s32[1024]{0:T(1024)S(1)} %dynamic_slice.32), kind=kLoop, calls=%fused_computation.9.clone.1 | loop fusion | flops 10483712 | bytes 8417280 | tf_op jit(solution)/shard_map/while/body/eval_jaxpr/reduce_sum | solution.py:72
  239.4 5.4 %fusion.49 = f32[1,88,2048]{2,1,0:T(8,128)S(1)} fusion(f32[1024,2048]{1,0:T(8,128)} %get-tuple-element.259, f32[2048]{0:T(1024)S(1)} %bitcast.112, s32[2048]{0:T(1024)S(1)} %get-tuple-element.292, s32[1024]{0:T(1024)S(1)} %dynamic_slice.32, f32[1,88,2048]{2,1,0:T(8,128)S(1)} %get-tuple-element.278, f32[2048]{0:T(1024)S(1)} %bitcast.119, ...), kind=kOutput, calls=%fused_computation.12.clone.1 | convolution fusion | flops 380125184 | bytes 10039305 | tf_op jit(solution)/shard_map/while/body/eval_jaxpr/hqk,hdk->hdq/dot_general | solution.py:73
  244.8 5.6 %fusion.45 = (f32[2048]{0:T(1024)S(1)}, f32[1024,2048]{1,0:T(8,128)}) fusion(s32[2048]{0:T(1024)S(1)} %get-tuple-element.292, s32[1024]{0:T(1024)S(1)} %dynamic_slice.32, bf16[1,88,2048]{2,1,0:T(8,128)(2,1)S(1)} %get-tuple-element.295, bf16[2,88,16384]{2,1,0:T(8,128)(2,1)} %get-tuple-element.294, s32[]{:T(128)S(6)} %select_n.132), kind=kOutput, calls=%fused_computation.5.clone.1 | convolution fusion | flops 377485312 | bytes 8949764 | tf_op jit(solution)/shard_map/while/body/eval_jaxpr/hdq,hdk->hqk/dot_general | solution.py:65
  250.4 4.8 %fusion.47 = f32[2048]{0:T(1024)S(1)} fusion(f32[1024,2048]{1,0:T(8,128)} %get-tuple-element.259, f32[2048]{0:T(1024)S(1)} %bitcast.111, s32[2048]{0:T(1024)S(1)} %get-tuple-element.292, s32[1024]{0:T(1024)S(1)} %dynamic_slice.32), kind=kLoop, calls=%fused_computation.9.clone.1 | loop fusion | flops 10483712 | bytes 8417280 | tf_op jit(solution)/shard_map/while/body/eval_jaxpr/reduce_sum | solution.py:72
  255.3 5.7 %fusion.49 = f32[1,88,2048]{2,1,0:T(8,128)S(1)} fusion(f32[1024,2048]{1,0:T(8,128)} %get-tuple-element.259, f32[2048]{0:T(1024)S(1)} %bitcast.112, s32[2048]{0:T(1024)S(1)} %get-tuple-element.292, s32[1024]{0:T(1024)S(1)} %dynamic_slice.32, f32[1,88,2048]{2,1,0:T(8,128)S(1)} %get-tuple-element.278, f32[2048]{0:T(1024)S(1)} %bitcast.119, ...), kind=kOutput, calls=%fused_computation.12.clone.1 | convolution fusion | flops 380125184 | bytes 10039305 | tf_op jit(solution)/shard_map/while/body/eval_jaxpr/hqk,hdk->hdq/dot_general | solution.py:73
  261.0 5.6 %fusion.45 = (f32[2048]{0:T(1024)S(1)}, f32[1024,2048]{1,0:T(8,128)}) fusion(s32[2048]{0:T(1024)S(1)} %get-tuple-element.292, s32[1024]{0:T(1024)S(1)} %dynamic_slice.32, bf16[1,88,2048]{2,1,0:T(8,128)(2,1)S(1)} %get-tuple-element.295, bf16[2,88,16384]{2,1,0:T(8,128)(2,1)} %get-tuple-element.294, s32[]{:T(128)S(6)} %select_n.132), kind=kOutput, calls=%fused_computation.5.clone.1 | convolution fusion | flops 377485312 | bytes 8949764 | tf_op jit(solution)/shard_map/while/body/eval_jaxpr/hdq,hdk->hqk/dot_general | solution.py:65
  266.6 4.8 %fusion.47 = f32[2048]{0:T(1024)S(1)} fusion(f32[1024,2048]{1,0:T(8,128)} %get-tuple-element.259, f32[2048]{0:T(1024)S(1)} %bitcast.111, s32[2048]{0:T(1024)S(1)} %get-tuple-element.292, s32[1024]{0:T(1024)S(1)} %dynamic_slice.32), kind=kLoop, calls=%fused_computation.9.clone.1 | loop fusion | flops 10483712 | bytes 8417280 | tf_op jit(solution)/shard_map/while/body/eval_jaxpr/reduce_sum | solution.py:72
  271.4 5.7 %fusion.49 = f32[1,88,2048]{2,1,0:T(8,128)S(1)} fusion(f32[1024,2048]{1,0:T(8,128)} %get-tuple-element.259, f32[2048]{0:T(1024)S(1)} %bitcast.112, s32[2048]{0:T(1024)S(1)} %get-tuple-element.292, s32[1024]{0:T(1024)S(1)} %dynamic_slice.32, f32[1,88,2048]{2,1,0:T(8,128)S(1)} %get-tuple-element.278, f32[2048]{0:T(1024)S(1)} %bitcast.119, ...), kind=kOutput, calls=%fused_computation.12.clone.1 | convolution fusion | flops 380125184 | bytes 10039305 | tf_op jit(solution)/shard_map/while/body/eval_jaxpr/hqk,hdk->hdq/dot_general | solution.py:73
  277.1 5.6 %fusion.45 = (f32[2048]{0:T(1024)S(1)}, f32[1024,2048]{1,0:T(8,128)}) fusion(s32[2048]{0:T(1024)S(1)} %get-tuple-element.292, s32[1024]{0:T(1024)S(1)} %dynamic_slice.32, bf16[1,88,2048]{2,1,0:T(8,128)(2,1)S(1)} %get-tuple-element.295, bf16[2,88,16384]{2,1,0:T(8,128)(2,1)} %get-tuple-element.294, s32[]{:T(128)S(6)} %select_n.132), kind=kOutput, calls=%fused_computation.5.clone.1 | convolution fusion | flops 377485312 | bytes 8949764 | tf_op jit(solution)/shard_map/while/body/eval_jaxpr/hdq,hdk->hqk/dot_general | solution.py:65
  287.5 5.4 %fusion.49 = f32[1,88,2048]{2,1,0:T(8,128)S(1)} fusion(f32[1024,2048]{1,0:T(8,128)} %get-tuple-element.259, f32[2048]{0:T(1024)S(1)} %bitcast.112, s32[2048]{0:T(1024)S(1)} %get-tuple-element.292, s32[1024]{0:T(1024)S(1)} %dynamic_slice.32, f32[1,88,2048]{2,1,0:T(8,128)S(1)} %get-tuple-element.278, f32[2048]{0:T(1024)S(1)} %bitcast.119, ...), kind=kOutput, calls=%fused_computation.12.clone.1 | convolution fusion | flops 380125184 | bytes 10039305 | tf_op jit(solution)/shard_map/while/body/eval_jaxpr/hqk,hdk->hdq/dot_general | solution.py:73
  293.0 5.6 %fusion.45 = (f32[2048]{0:T(1024)S(1)}, f32[1024,2048]{1,0:T(8,128)}) fusion(s32[2048]{0:T(1024)S(1)} %get-tuple-element.292, s32[1024]{0:T(1024)S(1)} %dynamic_slice.32, bf16[1,88,2048]{2,1,0:T(8,128)(2,1)S(1)} %get-tuple-element.295, bf16[2,88,16384]{2,1,0:T(8,128)(2,1)} %get-tuple-element.294, s32[]{:T(128)S(6)} %select_n.132), kind=kOutput, calls=%fused_computation.5.clone.1 | convolution fusion | flops 377485312 | bytes 8949764 | tf_op jit(solution)/shard_map/while/body/eval_jaxpr/hdq,hdk->hqk/dot_general | solution.py:65
  303.2 5.4 %fusion.49 = f32[1,88,2048]{2,1,0:T(8,128)S(1)} fusion(f32[1024,2048]{1,0:T(8,128)} %get-tuple-element.259, f32[2048]{0:T(1024)S(1)} %bitcast.112, s32[2048]{0:T(1024)S(1)} %get-tuple-element.292, s32[1024]{0:T(1024)S(1)} %dynamic_slice.32, f32[1,88,2048]{2,1,0:T(8,128)S(1)} %get-tuple-element.278, f32[2048]{0:T(1024)S(1)} %bitcast.119, ...), kind=kOutput, calls=%fused_computation.12.clone.1 | convolution fusion | flops 380125184 | bytes 10039305 | tf_op jit(solution)/shard_map/while/body/eval_jaxpr/hqk,hdk->hdq/dot_general | solution.py:73
  308.6 5.6 %fusion.45 = (f32[2048]{0:T(1024)S(1)}, f32[1024,2048]{1,0:T(8,128)}) fusion(s32[2048]{0:T(1024)S(1)} %get-tuple-element.292, s32[1024]{0:T(1024)S(1)} %dynamic_slice.32, bf16[1,88,2048]{2,1,0:T(8,128)(2,1)S(1)} %get-tuple-element.295, bf16[2,88,16384]{2,1,0:T(8,128)(2,1)} %get-tuple-element.294, s32[]{:T(128)S(6)} %select_n.132), kind=kOutput, calls=%fused_computation.5.clone.1 | convolution fusion | flops 377485312 | bytes 8949764 | tf_op jit(solution)/shard_map/while/body/eval_jaxpr/hdq,hdk->hqk/dot_general | solution.py:65
  318.8 5.4 %fusion.49 = f32[1,88,2048]{2,1,0:T(8,128)S(1)} fusion(f32[1024,2048]{1,0:T(8,128)} %get-tuple-element.259, f32[2048]{0:T(1024)S(1)} %bitcast.112, s32[2048]{0:T(1024)S(1)} %get-tuple-element.292, s32[1024]{0:T(1024)S(1)} %dynamic_slice.32, f32[1,88,2048]{2,1,0:T(8,128)S(1)} %get-tuple-element.278, f32[2048]{0:T(1024)S(1)} %bitcast.119, ...), kind=kOutput, calls=%fused_computation.12.clone.1 | convolution fusion | flops 380125184 | bytes 10039305 | tf_op jit(solution)/shard_map/while/body/eval_jaxpr/hqk,hdk->hdq/dot_general | solution.py:73
  324.3 5.6 %fusion.45 = (f32[2048]{0:T(1024)S(1)}, f32[1024,2048]{1,0:T(8,128)}) fusion(s32[2048]{0:T(1024)S(1)} %get-tuple-element.292, s32[1024]{0:T(1024)S(1)} %dynamic_slice.32, bf16[1,88,2048]{2,1,0:T(8,128)(2,1)S(1)} %get-tuple-element.295, bf16[2,88,16384]{2,1,0:T(8,128)(2,1)} %get-tuple-element.294, s32[]{:T(128)S(6)} %select_n.132), kind=kOutput, calls=%fused_computation.5.clone.1 | convolution fusion | flops 377485312 | bytes 8949764 | tf_op jit(solution)/shard_map/while/body/eval_jaxpr/hdq,hdk->hqk/dot_general | solution.py:65
  334.5 5.4 %fusion.49 = f32[1,88,2048]{2,1,0:T(8,128)S(1)} fusion(f32[1024,2048]{1,0:T(8,128)} %get-tuple-element.259, f32[2048]{0:T(1024)S(1)} %bitcast.112, s32[2048]{0:T(1024)S(1)} %get-tuple-element.292, s32[1024]{0:T(1024)S(1)} %dynamic_slice.32, f32[1,88,2048]{2,1,0:T(8,128)S(1)} %get-tuple-element.278, f32[2048]{0:T(1024)S(1)} %bitcast.119, ...), kind=kOutput, calls=%fused_computation.12.clone.1 | convolution fusion | flops 380125184 | bytes 10039305 | tf_op jit(solution)/shard_map/while/body/eval_jaxpr/hqk,hdk->hdq/dot_general | solution.py:73
  339.9 5.6 %fusion.45 = (f32[2048]{0:T(1024)S(1)}, f32[1024,2048]{1,0:T(8,128)}) fusion(s32[2048]{0:T(1024)S(1)} %get-tuple-element.292, s32[1024]{0:T(1024)S(1)} %dynamic_slice.32, bf16[1,88,2048]{2,1,0:T(8,128)(2,1)S(1)} %get-tuple-element.295, bf16[2,88,16384]{2,1,0:T(8,128)(2,1)} %get-tuple-element.294, s32[]{:T(128)S(6)} %select_n.132), kind=kOutput, calls=%fused_computation.5.clone.1 | convolution fusion | flops 377485312 | bytes 8949764 | tf_op jit(solution)/shard_map/while/body/eval_jaxpr/hdq,hdk->hqk/dot_general | solution.py:65
  350.2 5.4 %fusion.49 = f32[1,88,2048]{2,1,0:T(8,128)S(1)} fusion(f32[1024,2048]{1,0:T(8,128)} %get-tuple-element.259, f32[2048]{0:T(1024)S(1)} %bitcast.112, s32[2048]{0:T(1024)S(1)} %get-tuple-element.292, s32[1024]{0:T(1024)S(1)} %dynamic_slice.32, f32[1,88,2048]{2,1,0:T(8,128)S(1)} %get-tuple-element.278, f32[2048]{0:T(1024)S(1)} %bitcast.119, ...), kind=kOutput, calls=%fused_computation.12.clone.1 | convolution fusion | flops 380125184 | bytes 10039305 | tf_op jit(solution)/shard_map/while/body/eval_jaxpr/hqk,hdk->hdq/dot_general | solution.py:73
  355.6 5.6 %fusion.45 = (f32[2048]{0:T(1024)S(1)}, f32[1024,2048]{1,0:T(8,128)}) fusion(s32[2048]{0:T(1024)S(1)} %get-tuple-element.292, s32[1024]{0:T(1024)S(1)} %dynamic_slice.32, bf16[1,88,2048]{2,1,0:T(8,128)(2,1)S(1)} %get-tuple-element.295, bf16[2,88,16384]{2,1,0:T(8,128)(2,1)} %get-tuple-element.294, s32[]{:T(128)S(6)} %select_n.132), kind=kOutput, calls=%fused_computation.5.clone.1 | convolution fusion | flops 377485312 | bytes 8949764 | tf_op jit(solution)/shard_map/while/body/eval_jaxpr/hdq,hdk->hqk/dot_general | solution.py:65
  365.8 5.4 %fusion.49 = f32[1,88,2048]{2,1,0:T(8,128)S(1)} fusion(f32[1024,2048]{1,0:T(8,128)} %get-tuple-element.259, f32[2048]{0:T(1024)S(1)} %bitcast.112, s32[2048]{0:T(1024)S(1)} %get-tuple-element.292, s32[1024]{0:T(1024)S(1)} %dynamic_slice.32, f32[1,88,2048]{2,1,0:T(8,128)S(1)} %get-tuple-element.278, f32[2048]{0:T(1024)S(1)} %bitcast.119, ...), kind=kOutput, calls=%fused_computation.12.clone.1 | convolution fusion | flops 380125184 | bytes 10039305 | tf_op jit(solution)/shard_map/while/body/eval_jaxpr/hqk,hdk->hdq/dot_general | solution.py:73
  371.3 5.6 %fusion.45 = (f32[2048]{0:T(1024)S(1)}, f32[1024,2048]{1,0:T(8,128)}) fusion(s32[2048]{0:T(1024)S(1)} %get-tuple-element.292, s32[1024]{0:T(1024)S(1)} %dynamic_slice.32, bf16[1,88,2048]{2,1,0:T(8,128)(2,1)S(1)} %get-tuple-element.295, bf16[2,88,16384]{2,1,0:T(8,128)(2,1)} %get-tuple-element.294, s32[]{:T(128)S(6)} %select_n.132), kind=kOutput, calls=%fused_computation.5.clone.1 | convolution fusion | flops 377485312 | bytes 8949764 | tf_op jit(solution)/shard_map/while/body/eval_jaxpr/hdq,hdk->hqk/dot_general | solution.py:65
  381.5 5.4 %fusion.49 = f32[1,88,2048]{2,1,0:T(8,128)S(1)} fusion(f32[1024,2048]{1,0:T(8,128)} %get-tuple-element.259, f32[2048]{0:T(1024)S(1)} %bitcast.112, s32[2048]{0:T(1024)S(1)} %get-tuple-element.292, s32[1024]{0:T(1024)S(1)} %dynamic_slice.32, f32[1,88,2048]{2,1,0:T(8,128)S(1)} %get-tuple-element.278, f32[2048]{0:T(1024)S(1)} %bitcast.119, ...), kind=kOutput, calls=%fused_computation.12.clone.1 | convolution fusion | flops 380125184 | bytes 10039305 | tf_op jit(solution)/shard_map/while/body/eval_jaxpr/hqk,hdk->hdq/dot_general | solution.py:73
  386.9 5.6 %fusion.45 = (f32[2048]{0:T(1024)S(1)}, f32[1024,2048]{1,0:T(8,128)}) fusion(s32[2048]{0:T(1024)S(1)} %get-tuple-element.292, s32[1024]{0:T(1024)S(1)} %dynamic_slice.32, bf16[1,88,2048]{2,1,0:T(8,128)(2,1)S(1)} %get-tuple-element.295, bf16[2,88,16384]{2,1,0:T(8,128)(2,1)} %get-tuple-element.294, s32[]{:T(128)S(6)} %select_n.132), kind=kOutput, calls=%fused_computation.5.clone.1 | convolution fusion | flops 377485312 | bytes 8949764 | tf_op jit(solution)/shard_map/while/body/eval_jaxpr/hdq,hdk->hqk/dot_general | solution.py:65
  397.1 5.4 %fusion.49 = f32[1,88,2048]{2,1,0:T(8,128)S(1)} fusion(f32[1024,2048]{1,0:T(8,128)} %get-tuple-element.259, f32[2048]{0:T(1024)S(1)} %bitcast.112, s32[2048]{0:T(1024)S(1)} %get-tuple-element.292, s32[1024]{0:T(1024)S(1)} %dynamic_slice.32, f32[1,88,2048]{2,1,0:T(8,128)S(1)} %get-tuple-element.278, f32[2048]{0:T(1024)S(1)} %bitcast.119, ...), kind=kOutput, calls=%fused_computation.12.clone.1 | convolution fusion | flops 380125184 | bytes 10039305 | tf_op jit(solution)/shard_map/while/body/eval_jaxpr/hqk,hdk->hdq/dot_general | solution.py:73
  403.6 6.1 %all-to-all-start = ((bf16[88,16,128]{2,0,1:T(8,128)(2,1)}), bf16[88,16,128]{2,0,1:T(8,128)(2,1)S(1)}, u32[]{:S(2)}, u32[]{:S(2)}) async-start(bf16[88,16,128]{2,0,1:T(8,128)(2,1)} %copy.32), calls=%async_computation | async-start | bytes 720896 | tf_op jit(solution)/shard_map/all_to_all | solution.py:102
  409.7 7.7 %convert_element_type.50 = f32[1408,2048]{0,1:T(8,128)} convert(bf16[1408,2048]{0,1:T(8,128)(2,1)} %copy.28) | non-fusion elementwise | flops 2883584 | bytes 17301504 | tf_op jit(solution)/shard_map/convert_element_type | solution.py:33
  423.1 8.1 %fusion.23 = bf16[32,1408]{1,0:T(8,128)(2,1)S(1)} fusion(bf16[4,1408,1408]{2,1,0:T(8,128)(2,1)} %all-gather.11.cloned.1.call-done, bf16[1408,32,4]{0,2,1:T(4,128)(2,1)S(1)} %reshape.217), kind=kOutput, calls=%fused_computation.36 | convolution fusion | flops 507555840 | bytes 16310272 | tf_op jit(solution)/shard_map/fgi,ifd->gd/dot_general | solution.py:118
  432.5 5.0 %all-to-all-start.1 = ((bf16[16,32,1408]{2,1,0:T(8,128)(2,1)}), bf16[16,32,1408]{2,1,0:T(8,128)(2,1)S(1)}, u32[]{:S(2)}, u32[]{:S(2)}) async-start(bf16[16,32,1408]{2,1,0:T(8,128)(2,1)} %stack.2), calls=%async_computation.1 | async-start | bytes 2883584 | tf_op jit(solution)/shard_map/all_to_all | solution.py:120
  438.9 20.5 %all-to-all-done.1 = bf16[16,32,1408]{2,1,0:T(8,128)(2,1)S(1)} async-done(((bf16[16,32,1408]{2,1,0:T(8,128)(2,1)}), bf16[16,32,1408]{2,1,0:T(8,128)(2,1)S(1)}, u32[]{:S(2)}, u32[]{:S(2)}) %all-to-all-start.1) | async-done | bytes 1441824 | tf_op jit(solution)/shard_map/all_to_all | solution.py:120
  (132 shorter events, 90.6 us)
Async XLA Ops:
  6.5 86.1 %copy-start = (bf16[2,88,1408]{2,1,0:T(8,128)(2,1)S(1)}, bf16[2,88,1408]{2,1,0:T(8,128)(2,1)}, u32[]{:S(2)}) copy-start(bf16[2,88,1408]{2,1,0:T(8,128)(2,1)} %param.16) | copy-start | bytes 1486852
  6.5 64.2 %all-gather.5.cloned.1.call-start = ((), (), s32[]{:S(2)}) async-start(), calls=%async_computation.2 | async-start | bytes 6127616 | tf_op jit(solution)/shard_map/all_gather | solution.py:31
  7.3 134.5 %all-gather.7.cloned.1.call-start = ((), (), s32[]{:S(2)}) async-start(), calls=%async_computation.3 | async-start | bytes 6782976 | tf_op jit(solution)/shard_map/all_gather | solution.py:56
  79.1 4.5 copy-start.2
  87.6 15.2 %copy-start.4 = (bf16[88,1408]{1,0:T(8,128)(2,1)S(1)}, bf16[88,1408]{1,0:T(8,128)(2,1)}, u32[]{:S(2)}) copy-start(bf16[88,1408]{1,0:T(8,128)(2,1)} %param.15) | copy-start | bytes 743428
  101.8 315.5 %all-gather.9.cloned.1.call-start = ((), (), s32[]{:S(2)}) async-start(), calls=%async_computation.4 | async-start | bytes 4212736 | tf_op jit(solution)/shard_map/all_gather | solution.py:32
  102.6 320.6 %all-gather.11.cloned.1.call-start = ((), (), s32[]{:S(2)}) async-start(), calls=%async_computation.5 | async-start | bytes 16850944 | tf_op jit(solution)/shard_map/all_gather | solution.py:116
  102.8 45.7 %copy-start.3 = (s32[2048]{0:T(1024)S(1)}, s32[2048]{0:T(1024)}, u32[]{:S(2)}) copy-start(s32[2048]{0:T(1024)} %param.19) | copy-start | bytes 24580
  148.5 261.1 %copy-start.5 = (bf16[1408]{0:T(1024)(128)(2,1)S(1)}, bf16[1408]{0:T(1024)(128)(2,1)}, u32[]{:S(2)}) copy-start(bf16[1408]{0:T(1024)(128)(2,1)} %param.21) | copy-start | bytes 8452
  403.6 16.0 %all-to-all-start = ((bf16[88,16,128]{2,0,1:T(8,128)(2,1)}), bf16[88,16,128]{2,0,1:T(8,128)(2,1)S(1)}, u32[]{:S(2)}, u32[]{:S(2)}) async-start(bf16[88,16,128]{2,0,1:T(8,128)(2,1)} %copy.32), calls=%async_computation | async-start | bytes 720896 | tf_op jit(solution)/shard_map/all_to_all | solution.py:102
  423.0 38.0 %copy-start.1 = (bf16[2,88,1408]{2,1,0:T(8,128)(2,1)S(1)}, bf16[2,88,1408]{2,1,0:T(8,128)(2,1)}, u32[]{:S(2)}) copy-start(bf16[2,88,1408]{2,1,0:T(8,128)(2,1)} %param.16) | copy-start | bytes 1486852
  432.5 26.9 %all-to-all-start.1 = ((bf16[16,32,1408]{2,1,0:T(8,128)(2,1)}), bf16[16,32,1408]{2,1,0:T(8,128)(2,1)S(1)}, u32[]{:S(2)}, u32[]{:S(2)}) async-start(bf16[16,32,1408]{2,1,0:T(8,128)(2,1)} %stack.2), calls=%async_computation.1 | async-start | bytes 2883584 | tf_op jit(solution)/shard_map/all_to_all | solution.py:120
Sparse Core Ops, SparseCore 0:
  9.5 61.1 all-gather.4
  101.9 39.7 all-gather.6
  143.9 50.4 all-gather.8
  196.4 106.0 all-gather.10
